TPU v7x, 128 devices: a whole 4x4x4 slice. The times are simulated.
128 devices in a mesh: row: 8 (over y, core), col: 16 (over z, x).
Axes of the slice: x: 4, y: 4, z: 4, core: 2. Of those that a mesh axis runs over, the one named last changes fastest.
Arguments:
- hidden_states: bfloat16 [1024, 2048], P('col', 'row'), may hold values from -20 to 20
- input_gain: float32 [2, 2048], P(None, 'row'), may hold values from 0.25 to 1.75
- inner_weight: bfloat16 [2, 2048, 2, 4096], P(None, 'row', None, 'col'), may hold values from -0.125 to 0.125
- proj_weight: bfloat16 [2, 2048, 256], P(None, 'row'), may hold values from -0.125 to 0.125
- step_weight: bfloat16 [2, 2048, 64], P(None, 'row', 'col'), may hold values from -0.125 to 0.125
- inner_kernel: float32 [2, 4, 4096], P(None, None, 'col'), may hold values from -3 to 3
- proj_kernel: float32 [2, 4, 256], replicated, may hold values from -3 to 3
- step_bias: float32 [2, 64], P(None, 'col'), may hold values from -5 to -1
- decay_log: float32 [2, 64], P(None, 'col'), may hold values from -2 to 1
- skip_gain: float32 [2, 64], P(None, 'col'), may hold values from 0.5 to 1.5
- norm_gain: float32 [2, 4096], P(None, 'col'), may hold values from 0.25 to 1.75
- out_weight: bfloat16 [2, 4096, 2048], P(None, 'col', 'row'), may hold values from -0.09375 to 0.09375
- inner_cache: bfloat16 [2, 64, 3, 4096], P(None, 'row', None, 'col'), may hold values from -6 to 6
- proj_cache: bfloat16 [2, 64, 3, 256], P(None, 'row'), may hold values from -6 to 6
- state_cache: float32 [2, 64, 64, 64, 128], P(None, 'row', 'col'), may hold values from -1.2 to 1.2
- accepted: int32 [64], P('row'), may hold values from 1 to 16
- owners: int32 [64], P('row'), may hold values from 0 to 15, as said below
- tenant_ranges: int32 [4, 2], replicated, may hold values from 0 to 64, as said below
Outputs:
- hidden_output: bfloat16 [1024, 2048], P('col', 'row')
- step_states: bfloat16 [2, 64, 16, 64, 64, 128], P(None, 'row', None, 'col')
- owned_states: bfloat16 [8, 16, 2, 2, 64, 64, 128], P('row', 'col')
Inputs may be any that keep to these rules, and one draw needn't show every extreme that they name: `owners`: within the requests of one index of row (aligned blocks of 8) no owner appears more than 2 times, and in every block some owner appears exactly 2 times. `tenant_ranges`: the ranges are in order, disjoint and not empty; exactly 8 requests lie in no range.
All inputs are finite; a program needn't handle non-finite values.
Results may differ from a plain program's by a relative error of at most 0.024.
Values may be sent and summed in bfloat16 or wider, within the bound.
No kernel may reach another device: no remote copies, remote signals or barrier semaphores. Data moves between devices by JAX's collectives and lax.ppermute only.
A program may use at most 128 MiB of HBM per device.

v0:
```python
import jax
import jax.numpy as jnp
from jax import lax
from jax.sharding import PartitionSpec as P

S = 16
SEND_CAP = 2
EPSILON = 1e-05


def conv_silu(prefix, incoming, kernel):
    joined = jnp.concatenate([prefix, incoming], axis=1)
    length = incoming.shape[1]
    summed = joined[:, 0:length, :] * kernel[0]
    for offset in range(1, kernel.shape[0]):
        summed = summed + joined[:, offset : offset + length, :] * kernel[offset]
    return jax.nn.silu(summed)


def ssm_scan(decays, deltas, inner_values, b_values, c_values, skip_values, start_state):

    def advance(carried, packed):
        decay_now, delta_now, value_now, b_now, c_now = packed
        updated = (
            decay_now[:, :, None, None] * carried
            + (delta_now[:, :, None] * value_now)[:, :, :, None] * b_now[:, None, None, :]
        )
        output = (
            jnp.einsum("rhpn,rn->rhp", updated, c_now, precision=lax.Precision.HIGHEST)
            + skip_values[None, :, None] * value_now
        )
        return (updated, (output, updated.astype(jnp.bfloat16)))

    time_major = tuple(
        (
            jnp.moveaxis(member, 1, 0)
            for member in (decays, deltas, inner_values, b_values, c_values)
        )
    )
    last_state, (outputs, states) = lax.scan(advance, start_state, time_major)
    return (jnp.moveaxis(outputs, 0, 1), jnp.moveaxis(states, 0, 1))


def local(
    hidden_states,
    input_gain,
    inner_weight,
    proj_weight,
    step_weight,
    inner_kernel,
    proj_kernel,
    step_bias,
    decay_log,
    skip_gain,
    norm_gain,
    out_weight,
    inner_cache,
    proj_cache,
    state_cache,
    accepted,
    owners,
    tenant_ranges,
):
    layer_count = inner_weight.shape[0]
    row_width = inner_weight.shape[1]
    inner_local = inner_weight.shape[3]
    heads_local = step_weight.shape[2]
    head_size = inner_local // heads_local
    state_size = proj_weight.shape[2] // 2
    requests_local = state_cache.shape[1]
    draft_steps = S
    row_count = lax.axis_size("row")
    col_count = lax.axis_size("col")
    model_width = row_width * row_count
    inner_width = inner_local * col_count
    token_rows = requests_local * draft_steps
    local_ids = jnp.arange(requests_local, dtype=jnp.int32)
    request_ids = lax.axis_index("row") * requests_local + local_ids
    live_mask = jnp.any(
        (request_ids[:, None] >= tenant_ranges[None, :, 0])
        & (request_ids[:, None] < tenant_ranges[None, :, 1]),
        axis=1,
    )
    earlier = (owners[:, None] == owners[None, :]) & (local_ids[None, :] < local_ids[:, None])
    slot_ranks = jnp.sum(earlier.astype(jnp.int32), axis=1)
    slot_ids = owners * SEND_CAP + slot_ranks
    slot_grid = jnp.arange(col_count * SEND_CAP, dtype=jnp.int32)
    step_grid = jnp.arange(draft_steps, dtype=jnp.int32)
    picker = (
        (slot_grid[:, None, None] == slot_ids[None, :, None])
        & (step_grid[None, None, :] == accepted[None, :, None] - 1)
        & live_mask[None, :, None]
    )
    picker = picker.astype(jnp.bfloat16).reshape(col_count * SEND_CAP, token_rows)
    hidden = hidden_states
    step_outputs = []
    chosen_layers = []
    for layer_index in range(layer_count):
        all_tokens = lax.all_gather(hidden, "col", axis=0, tiled=True)
        tokens_f = all_tokens.astype(jnp.float32)
        scaled = (tokens_f * input_gain[layer_index]).astype(jnp.bfloat16)
        square_part = jnp.sum(tokens_f * tokens_f, axis=1)
        inner_part = jnp.dot(
            scaled,
            inner_weight[layer_index].reshape(row_width, 2 * inner_local),
            preferred_element_type=jnp.float32,
        )
        step_part = jnp.dot(scaled, step_weight[layer_index], preferred_element_type=jnp.float32)
        proj_part = jnp.dot(scaled, proj_weight[layer_index], preferred_element_type=jnp.float32)
        inner_sum, step_sum, proj_sum, square_sum = (
            lax.psum_scatter(inner_part, "row", scatter_dimension=0, tiled=True),
            lax.psum_scatter(step_part, "row", scatter_dimension=0, tiled=True),
            lax.psum_scatter(proj_part, "row", scatter_dimension=0, tiled=True),
            lax.psum_scatter(square_part, "row", scatter_dimension=0, tiled=True),
        )
        inverse_rms = lax.rsqrt(square_sum / model_width + EPSILON)
        inner_vals = inner_sum * inverse_rms[:, None]
        gate_vals = inner_vals[:, :inner_local]
        raw_inner = inner_vals[:, inner_local:].reshape(requests_local, draft_steps, inner_local)
        raw_proj = (proj_sum * inverse_rms[:, None]).reshape(
            requests_local, draft_steps, 2 * state_size
        )
        conv_inner = conv_silu(
            inner_cache[layer_index].astype(jnp.float32), raw_inner, inner_kernel[layer_index]
        )
        conv_proj = conv_silu(
            proj_cache[layer_index].astype(jnp.float32), raw_proj, proj_kernel[layer_index]
        )
        deltas = jax.nn.softplus(
            (step_sum * inverse_rms[:, None]).reshape(requests_local, draft_steps, heads_local)
            + step_bias[layer_index]
        )
        decays = jnp.exp(-deltas * jnp.exp(decay_log[layer_index]))
        outputs, states = ssm_scan(
            decays,
            deltas,
            conv_inner.reshape(requests_local, draft_steps, heads_local, head_size),
            conv_proj[..., :state_size],
            conv_proj[..., state_size:],
            skip_gain[layer_index],
            state_cache[layer_index],
        )
        step_outputs.append(states)
        gated_raw = outputs.reshape(token_rows, inner_local) * jax.nn.silu(gate_vals)
        gate_square = lax.psum(jnp.sum(gated_raw * gated_raw, axis=1), "col")
        gated = (
            gated_raw
            * norm_gain[layer_index]
            * lax.rsqrt(gate_square / inner_width + EPSILON)[:, None]
        ).astype(jnp.bfloat16)
        layer_weight = out_weight[layer_index]
        partial_out = jnp.dot(
            lax.all_gather(gated, "row", axis=0, tiled=True),
            layer_weight,
            preferred_element_type=jnp.float32,
        )
        out_sum = lax.psum_scatter(
            partial_out.astype(jnp.bfloat16), "col", scatter_dimension=0, tiled=True
        ).astype(jnp.float32)
        hidden = (hidden.astype(jnp.float32) + out_sum).astype(jnp.bfloat16)
        chosen = jnp.dot(
            picker,
            states.reshape(token_rows, heads_local * head_size * state_size),
            preferred_element_type=jnp.float32,
        )
        chosen = chosen.astype(jnp.bfloat16).reshape(
            col_count, SEND_CAP, heads_local, head_size, state_size
        )
        chosen_layers.append(chosen)
    gathered = lax.all_to_all(
        jnp.stack(chosen_layers, axis=2), "col", split_axis=0, concat_axis=3, tiled=True
    )
    owned_block = gathered[None]
    step_all = jnp.stack(step_outputs, axis=0)
    return (hidden, step_all, owned_block)


def solution(mesh):
    placed = (
        P("col", "row"),
        P(None, "row"),
        P(None, "row", None, "col"),
        P(None, "row", None),
        P(None, "row", "col"),
        P(None, None, "col"),
        P(),
        P(None, "col"),
        P(None, "col"),
        P(None, "col"),
        P(None, "col"),
        P(None, "col", "row"),
        P(None, "row", None, "col"),
        P(None, "row", None, None),
        P(None, "row", "col", None, None),
        P("row"),
        P("row"),
        P(),
    )
    return jax.shard_map(
        local,
        mesh=mesh,
        in_specs=placed,
        out_specs=(
            P("col", "row"),
            P(None, "row", None, "col", None, None),
            P("row", "col", None, None, None, None, None),
        ),
        check_vma=False,
    )
```

profile of v0, /device:TPU:0, one launch (start us, length us, event | category | flops | bytes accessed | tf_op | source)
XLA Modules:
  0.0 788.9 jit_solution(10721165272953729870)
XLA Ops:
  8.6 25.4 %all_gather.12 = bf16[1024,256]{1,0:T(8,128)(2,1)S(1)} all-gather(bf16[64,256]{1,0:T(8,128)(2,1)} %param.22), channel_id=1, replica_groups=mesh['row'=8,'col'=16] {'col'}, dimensions={0}, use_global_device_ids=true | all-gather | bytes 557056 | tf_op jit(solution)/shard_map/all_gather | solution.py:99
  34.1 1.8 fusion.18
  35.9 2.2 fusion.14
  42.9 12.5 %all-reduce = f32[1024]{0:T(1024)S(1)} all-reduce(f32[1024]{0:T(1024)S(1)} %fusion.5), channel_id=3, replica_groups=mesh['row'=8,'col'=16] {'row'}, use_global_device_ids=true, to_apply=%region_2.0.clone | all-reduce | flops 1024 | bytes 8192
  60.8 5.6 reduce-scatter.25.cloned.1.call-done
  69.0 31.3 %reduce-scatter.15.cloned.1.call-done = f32[128,256]{1,0:T(8,128)} async-done(((f32[1024,256]{1,0:T(8,128)}), f32[128,256]{1,0:T(8,128)}) %reduce-scatter.15.cloned.1.call-update) | async-done | bytes 131088 | tf_op jit(solution)/shard_map/reduce_scatter | solution.py:113
  102.1 33.8 %reduce-scatter.13.cloned.1.call-done = f32[128,512]{1,0:T(8,128)} async-done(((f32[1024,512]{1,0:T(8,128)}), f32[128,512]{1,0:T(8,128)}) %reduce-scatter.13.cloned.1.call-update) | async-done | bytes 262160 | tf_op jit(solution)/shard_map/reduce_scatter | solution.py:111
  137.4 5.4 broadcast.153.clone2
  142.7 103.3 %while.28 = (s32[]{:T(128)}, f32[8,4,64,128]{3,2,1,0:T(8,128)S(1)}, f32[16,8,4,64]{3,2,1,0:T(4,128)S(1)}, bf16[16,8,4,64,128]{4,3,2,0,1:T(8,128)(2,1)}, f32[16,8...) while((s32[]{:T(128)}, f32[8,4,64,128]{3,2,1,0:T(8,128)S(1)}, ...), condition=%wide.region_6.0_spmd, body=%wide.region_5.0_spmd.sunk | while | flops 4200450 | bytes 3777949 | solution.py:40
  145.9 2.5 fusion.99
  152.4 2.5 fusion.99
  158.8 2.5 fusion.99
  165.3 2.5 fusion.99
  171.7 2.5 fusion.99
  178.2 2.5 fusion.99
  184.6 2.5 fusion.99
  191.1 2.5 fusion.99
  197.6 2.5 fusion.99
  204.0 2.5 fusion.99
  210.5 2.5 fusion.99
  216.9 2.5 fusion.99
  223.4 2.5 fusion.99
  229.8 2.5 fusion.99
  236.3 2.5 fusion.99
  242.8 2.5 fusion.99
  246.5 40.5 %psum.14 = f32[128]{0:T(128)S(1)} all-reduce(f32[128]{0:T(128)S(1)} %get-tuple-element.179), channel_id=1, replica_groups=mesh['row'=8,'col'=16] {'col'}, use_global_device_ids=true, to_apply=%region_8.9 | all-reduce | flops 128 | bytes 1024 | tf_op jit(solution)/shard_map/psum | solution.py:145
  287.8 13.1 %all_gather.13 = bf16[1024,256]{1,0:T(8,128)(2,1)S(1)} all-gather(bf16[128,256]{1,0:T(8,128)(2,1)S(1)} %multiply_convert_fusion.1), channel_id=1, replica_groups=mesh['row'=8,'col'=16] {'row'}, dimensions={0}, use_global_device_ids=true | all-gather | bytes 589824 | tf_op jit(solution)/shard_map/all_gather | solution.py:153
  300.9 2.0 convolution_convert_fusion.3
  302.9 67.3 %reduce-scatter.17.cloned.1.call-done = bf16[64,256]{1,0:T(8,128)(2,1)} async-done(((bf16[1024,256]{1,0:T(8,128)(2,1)}), bf16[64,256]{1,0:T(8,128)(2,1)}) %reduce-scatter.17.cloned.1.call-update) | async-done | bytes 32784 | tf_op jit(solution)/shard_map/reduce_scatter | solution.py:157
  371.0 23.3 %all_gather.14 = bf16[1024,256]{1,0:T(8,128)(2,1)S(1)} all-gather(bf16[64,256]{1,0:T(8,128)(2,1)S(1)} %add_convert_fusion.1), channel_id=1, replica_groups=mesh['row'=8,'col'=16] {'col'}, dimensions={0}, use_global_device_ids=true | all-gather | bytes 557056 | tf_op jit(solution)/shard_map/all_gather | solution.py:99
  396.2 2.0 fusion.8
  400.6 13.3 %reshape.291 = bf16[128,32768]{1,0:T(8,128)(2,1)} reshape(bf16[8,16,4,64,128]{4,3,2,1,0:T(8,128)(2,1)} %bitcast.249) | data formatting | bytes 16777216 | tf_op jit(solution)/shard_map/reshape | solution.py:163
  414.0 4.7 fusion.2
  418.7 1.8 copy.158
  420.7 12.6 %all-reduce.1 = f32[1024]{0:T(1024)S(1)} all-reduce(f32[1024]{0:T(1024)S(1)} %fusion.7), channel_id=8, replica_groups=mesh['row'=8,'col'=16] {'row'}, use_global_device_ids=true, to_apply=%region_12.13.clone | all-reduce | flops 1024 | bytes 8192
  434.7 24.2 %reduce-scatter.21.cloned.1.call-done = f32[128,256]{1,0:T(8,128)} async-done(((f32[1024,256]{1,0:T(8,128)}), f32[128,256]{1,0:T(8,128)}) %reduce-scatter.21.cloned.1.call-update) | async-done | bytes 131088 | tf_op jit(solution)/shard_map/reduce_scatter | solution.py:113
  460.1 34.4 %reduce-scatter.19.cloned.1.call-done = f32[128,512]{1,0:T(8,128)} async-done(((f32[1024,512]{1,0:T(8,128)}), f32[128,512]{1,0:T(8,128)}) %reduce-scatter.19.cloned.1.call-update) | async-done | bytes 262160 | tf_op jit(solution)/shard_map/reduce_scatter | solution.py:111
  496.0 5.4 broadcast.153.clone
  501.4 70.9 %while.29 = (s32[]{:T(128)}, f32[8,4,64,128]{3,2,1,0:T(8,128)S(1)}, f32[16,8,4,64]{3,2,1,0:T(4,128)S(1)}, bf16[16,8,4,64,128]{4,3,2,0,1:T(8,128)(2,1)}, f32[16,8...) while((s32[]{:T(128)}, f32[8,4,64,128]{3,2,1,0:T(8,128)S(1)}, ...), condition=%wide.region_16.17_spmd, body=%wide.region_15.16_spmd.sunk | while | flops 4200450 | bytes 3778445 | solution.py:40
  503.2 2.5 fusion.102
  507.6 2.5 fusion.102
  512.1 2.5 fusion.102
  516.5 2.5 fusion.102
  520.9 2.5 fusion.102
  525.4 2.5 fusion.102
  529.8 2.5 fusion.102
  534.2 2.5 fusion.102
  538.7 2.5 fusion.102
  543.1 2.5 fusion.102
  547.6 2.5 fusion.102
  552.0 2.5 fusion.102
  556.5 2.5 fusion.102
  560.9 2.5 fusion.102
  565.3 2.5 fusion.102
  569.7 2.5 fusion.102
  572.4 13.3 %reshape.292 = bf16[128,32768]{1,0:T(8,128)(2,1)} reshape(bf16[8,16,4,64,128]{4,3,2,1,0:T(8,128)(2,1)} %bitcast.247) | data formatting | bytes 16777216 | tf_op jit(solution)/shard_map/reshape | solution.py:163
  585.6 4.8 fusion.3
  591.0 2.4 pad_maximum_fusion.1
  593.3 7.0 all-to-all-start
  600.8 81.9 %psum.15 = f32[128]{0:T(128)S(1)} all-reduce(f32[128]{0:T(128)S(1)} %get-tuple-element.177), channel_id=1, replica_groups=mesh['row'=8,'col'=16] {'col'}, use_global_device_ids=true, to_apply=%region_18.19 | all-reduce | flops 128 | bytes 1024 | tf_op jit(solution)/shard_map/psum | solution.py:145
  682.8 21.8 %all_gather.15 = bf16[1024,256]{1,0:T(8,128)(2,1)S(1)} all-gather(bf16[128,256]{1,0:T(8,128)(2,1)S(1)} %multiply_convert_fusion), channel_id=1, replica_groups=mesh['row'=8,'col'=16] {'row'}, dimensions={0}, use_global_device_ids=true | all-gather | bytes 589824 | tf_op jit(solution)/shard_map/all_gather | solution.py:153
  705.7 13.8 %pad_maximum_fusion = bf16[2,8,16,4,64,128]{5,4,3,2,1,0:T(8,128)(2,1)} fusion(bf16[1,8,16,4,64,128]{5,4,3,2,1,0:T(8,128)(2,1)} %bitcast.248, bf16[1,8,16,4,64,128]{5,4,3,2,1,0:T(8,128)(2,1)} %bitcast.250), kind=kLoop, calls=%fused_computation.22 | loop fusion | flops 8388608 | bytes 33554432 | tf_op jit(solution)/shard_map/stack | solution.py:174
  719.5 55.1 %reduce-scatter.23.cloned.1.call-done = bf16[64,256]{1,0:T(8,128)(2,1)} async-done(((bf16[1024,256]{1,0:T(8,128)(2,1)}), bf16[64,256]{1,0:T(8,128)(2,1)}) %reduce-scatter.23.cloned.1.call-update) | async-done | bytes 32784 | tf_op jit(solution)/shard_map/reduce_scatter | solution.py:157
  776.1 6.0 copy.143
  (407 shorter events, 123.2 us)
Async XLA Ops:
  7.2 34.3 %copy-start.28 = (u32[128]{0:T(128)S(1)}, u32[128]{0:T(128)}, u32[]{:S(2)}) copy-start(u32[128]{0:T(128)} %constant.80) | copy-start | bytes 1540
  7.2 48.3 %copy-start.22 = (f32[2,4]{1,0:T(2,128)S(1)}, f32[2,4]{1,0:T(2,128)}, u32[]{:S(2)}) copy-start(f32[2,4]{1,0:T(2,128)} %param.31) | copy-start | bytes 100
  7.2 48.9 %copy-start.21 = (f32[2,256]{1,0:T(2,128)S(1)}, f32[2,256]{1,0:T(2,128)}, u32[]{:S(2)}) copy-start(f32[2,256]{1,0:T(2,128)} %param.32) | copy-start | bytes 6148
  7.2 49.5 %copy-start.25 = (f32[2,4]{1,0:T(2,128)S(1)}, f32[2,4]{1,0:T(2,128)}, u32[]{:S(2)}) copy-start(f32[2,4]{1,0:T(2,128)} %param.30) | copy-start | bytes 100
  7.2 49.5 %copy-start.24 = (f32[2,4]{1,0:T(2,128)S(1)}, f32[2,4]{1,0:T(2,128)}, u32[]{:S(2)}) copy-start(f32[2,4]{1,0:T(2,128)} %param.29) | copy-start | bytes 100
  7.2 50.0 %copy-start.8 = (f32[2,4,256]{2,1,0:T(4,128)S(1)}, f32[2,4,256]{2,1,0:T(4,128)}, u32[]{:S(2)}) copy-start(f32[2,4,256]{2,1,0:T(4,128)} %param.27) | copy-start | bytes 24580
  7.2 50.6 %copy-start.9 = (f32[2,4,256]{2,1,0:T(4,128)S(1)}, f32[2,4,256]{2,1,0:T(4,128)}, u32[]{:S(2)}) copy-start(f32[2,4,256]{2,1,0:T(4,128)} %param.28) | copy-start | bytes 24580
  7.2 51.2 %copy-start.5 = (bf16[2,8,3,256]{3,1,2,0:T(8,128)(2,1)S(1)}, bf16[2,8,3,256]{3,1,2,0:T(8,128)(2,1)}, u32[]{:S(2)}) copy-start(bf16[2,8,3,256]{3,1,2,0:T(8,128)(2,1)} %param.34) | copy-start | bytes 73732
  7.3 51.2 %copy-start.6 = (bf16[2,8,3,256]{3,1,2,0:T(8,128)(2,1)S(1)}, bf16[2,8,3,256]{3,1,2,0:T(8,128)(2,1)}, u32[]{:S(2)}) copy-start(bf16[2,8,3,256]{3,1,2,0:T(8,128)(2,1)} %param.35) | copy-start | bytes 73732
  7.3 59.2 %reduce-scatter.25.cloned.1.call-start = ((), (), s32[]{:S(2)}) async-start(), calls=%async_computation.15 | async-start | bytes 589824
  35.9 64.4 %reduce-scatter.15.cloned.1.call-start = ((), (), s32[]{:S(2)}) async-start(), calls=%async_computation.10 | async-start | bytes 1179648 | tf_op jit(solution)/shard_map/reduce_scatter | solution.py:113
  38.1 97.8 %reduce-scatter.13.cloned.1.call-start = ((), (), s32[]{:S(2)}) async-start(), calls=%async_computation.9 | async-start | bytes 2359296 | tf_op jit(solution)/shard_map/reduce_scatter | solution.py:111
  41.4 328.8 %reduce-scatter.17.cloned.1.call-start = ((), (), s32[]{:S(2)}) async-start(), calls=%async_computation.11 | async-start | bytes 557056 | tf_op jit(solution)/shard_map/reduce_scatter | solution.py:157
  142.7 227.5 %copy-start.3 = (bf16[64,256]{1,0:T(8,128)(2,1)S(1)}, bf16[64,256]{1,0:T(8,128)(2,1)}, u32[]{:S(2)}) copy-start(bf16[64,256]{1,0:T(8,128)(2,1)} %param.22) | copy-start | bytes 98308
  142.7 253.4 %copy-start.1 = (bf16[2,256,256]{2,1,0:T(8,128)(2,1)S(1)}, bf16[2,256,256]{2,1,0:T(8,128)(2,1)}, u32[]{:S(2)}) copy-start(bf16[2,256,256]{2,1,0:T(8,128)(2,1)} %param.25) | copy-start | bytes 786436
  246.1 152.2 %copy-start.7 = (f32[1,256]{1,0:T(1,128)S(1)}, f32[1,256]{1,0:T(1,128)}, u32[]{:S(2)}) copy-start(f32[1,256]{1,0:T(1,128)} %get-tuple-element.219) | copy-start | bytes 3076
  246.1 154.0 %copy-start.27 = (s32[8]{0:T(128)S(1)}, s32[8]{0:T(128)}, u32[]{:S(2)}) copy-start(s32[8]{0:T(128)} %param.38) | copy-start | bytes 100
  246.1 154.2 %copy-start.23 = (s32[4,2]{0,1:T(2,128)S(1)}, s32[4,2]{0,1:T(2,128)}, u32[]{:S(2)}) copy-start(s32[4,2]{0,1:T(2,128)} %param.39) | copy-start | bytes 100
  246.1 154.3 %copy-start.26 = (s32[8]{0:T(128)S(1)}, s32[8]{0:T(128)}, u32[]{:S(2)}) copy-start(s32[8]{0:T(128)} %param.37) | copy-start | bytes 100
  302.9 130.5 %reduce-scatter.27.cloned.1.call-start = ((), (), s32[]{:S(2)}) async-start(), calls=%async_computation.16 | async-start | bytes 589824
  396.1 62.8 %reduce-scatter.21.cloned.1.call-start = ((), (), s32[]{:S(2)}) async-start(), calls=%async_computation.13 | async-start | bytes 1179648 | tf_op jit(solution)/shard_map/reduce_scatter | solution.py:113
  398.2 96.4 %reduce-scatter.19.cloned.1.call-start = ((), (), s32[]{:S(2)}) async-start(), calls=%async_computation.12 | async-start | bytes 2359296 | tf_op jit(solution)/shard_map/reduce_scatter | solution.py:111
  413.9 20.5 %copy-start.19 = (f32[4]{0:T(128)S(1)}, f32[4]{0:T(128)}, u32[]{:S(2)}) copy-start(f32[4]{0:T(128)} %get-tuple-element.225) | copy-start | bytes 52
  413.9 20.5 %copy-start.20 = (f32[4]{0:T(128)S(1)}, f32[4]{0:T(128)}, u32[]{:S(2)}) copy-start(f32[4]{0:T(128)} %get-tuple-element.229) | copy-start | bytes 52
  413.9 46.1 %copy-start.4 = (f32[8,3,256]{2,0,1:T(8,128)S(1)}, f32[8,3,256]{2,0,1:T(8,128)}, u32[]{:S(2)}) copy-start(f32[8,3,256]{2,0,1:T(8,128)} %get-tuple-element.193) | copy-start | bytes 73732
  413.9 46.1 %copy-start.14 = (f32[1,1,256]{2,1,0:T(1,128)S(1)}, f32[1,1,256]{2,1,0:T(1,128)}, u32[]{:S(2)}) copy-start(f32[1,1,256]{2,1,0:T(1,128)} %get-tuple-element.201) | copy-start | bytes 3076
  413.9 46.1 %copy-start.15 = (f32[1,1,256]{2,1,0:T(1,128)S(1)}, f32[1,1,256]{2,1,0:T(1,128)}, u32[]{:S(2)}) copy-start(f32[1,1,256]{2,1,0:T(1,128)} %get-tuple-element.202) | copy-start | bytes 3076
  413.9 46.1 %copy-start.16 = (f32[1,1,256]{2,1,0:T(1,128)S(1)}, f32[1,1,256]{2,1,0:T(1,128)}, u32[]{:S(2)}) copy-start(f32[1,1,256]{2,1,0:T(1,128)} %get-tuple-element.207) | copy-start | bytes 3076
  413.9 46.1 %copy-start.17 = (f32[1,1,256]{2,1,0:T(1,128)S(1)}, f32[1,1,256]{2,1,0:T(1,128)}, u32[]{:S(2)}) copy-start(f32[1,1,256]{2,1,0:T(1,128)} %get-tuple-element.208) | copy-start | bytes 3076
  414.0 81.8 %copy-start.10 = (f32[1,1,256]{2,1,0:T(1,128)S(1)}, f32[1,1,256]{2,1,0:T(1,128)}, u32[]{:S(2)}) copy-start(f32[1,1,256]{2,1,0:T(1,128)} %get-tuple-element.209) | copy-start | bytes 3076
  414.0 81.8 %copy-start.11 = (f32[1,1,256]{2,1,0:T(1,128)S(1)}, f32[1,1,256]{2,1,0:T(1,128)}, u32[]{:S(2)}) copy-start(f32[1,1,256]{2,1,0:T(1,128)} %get-tuple-element.210) | copy-start | bytes 3076
  414.0 81.8 %copy-start.12 = (f32[1,1,256]{2,1,0:T(1,128)S(1)}, f32[1,1,256]{2,1,0:T(1,128)}, u32[]{:S(2)}) copy-start(f32[1,1,256]{2,1,0:T(1,128)} %get-tuple-element.215) | copy-start | bytes 3076
  414.0 81.8 %copy-start.13 = (f32[1,1,256]{2,1,0:T(1,128)S(1)}, f32[1,1,256]{2,1,0:T(1,128)}, u32[]{:S(2)}) copy-start(f32[1,1,256]{2,1,0:T(1,128)} %get-tuple-element.216) | copy-start | bytes 3076
  585.6 5.3 copy-start
  590.9 91.8 %copy-start.18 = (f32[1,256]{1,0:T(1,128)S(1)}, f32[1,256]{1,0:T(1,128)}, u32[]{:S(2)}) copy-start(f32[1,256]{1,0:T(1,128)} %get-tuple-element.217) | copy-start | bytes 3076
  590.9 113.7 %copy-start.2 = (bf16[2,256,256]{2,1,0:T(8,128)(2,1)S(1)}, bf16[2,256,256]{2,1,0:T(8,128)(2,1)}, u32[]{:S(2)}) copy-start(bf16[2,256,256]{2,1,0:T(8,128)(2,1)} %param.33) | copy-start | bytes 786436
  593.3 182.7 %all-to-all-start = ((bf16[16,2,2,4,64,128]{5,4,3,1,2,0:T(8,128)(2,1)}), bf16[16,2,2,4,64,128]{5,4,3,1,2,0:T(8,128)(2,1)}, u32[]{:S(2)}, u32[]{:S(2)}) async-start(bf16[16,2,2,4,64,128]{5,4,3,1,2,0:T(8,128)(2,1)} %pad_maximum_fusion.1), calls=%async_computation.6 | async-start | bytes 8388608 | tf_op jit(solution)/shard_map/all_to_all | solution.py:170
  600.3 174.4 %reduce-scatter.23.cloned.1.call-start = ((), (), s32[]{:S(2)}) async-start(), calls=%async_computation.14 | async-start | bytes 557056 | tf_op jit(solution)/shard_map/reduce_scatter | solution.py:157
Sparse Core Ops, SparseCore 0:
  36.0 30.4 reduce-scatter.24
  69.5 30.7 reduce-scatter.14
  103.4 32.4 reduce-scatter.12
  303.0 67.1 reduce-scatter.16
  396.2 29.5 reduce-scatter.26
  428.2 30.6 reduce-scatter.20
  462.0 32.5 reduce-scatter.18
  705.8 68.7 reduce-scatter.22
where the time goes:
time: 792 us; the launch traced here: 789 us
  waiting for transfers between devices  252 us (32%)
  blocking collectives  231 us (29%)
  matrix products  105 us (13%)
  other arithmetic  90.8 us (11%)
  local copies, waits for them, and re-layouts  86.9 us (11%)
  between operations  15.4 us (2%)
    psum x2, blocking collectives, local(): gate_square = lax.psum(jnp.sum(gated_raw * gated_raw, axis=1), 'col')  122 us
    reduce_scatter x2, waiting for transfers between devices, local(): lax.psum_scatter(partial_out.astype(jnp.bfloat16), 'col', scatter_dimensi...  122 us
    dot_general x32, matrix products, advance(): jnp.einsum('rhpn,rn->rhp', updated, c_now, precision=lax.Precision.HIGHEST)  80.9 us
    reduce_scatter x2, waiting for transfers between devices, local(): lax.psum_scatter(inner_part, 'row', scatter_dimension=0, tiled=True)  68.3 us
    dynamic_update_slice x64, other arithmetic, ssm_scan(): last_state, (outputs, states) = lax.scan(advance, start_state, time_major)  62.7 us
    reduce_scatter x2, waiting for transfers between devices, local(): lax.psum_scatter(proj_part, 'row', scatter_dimension=0, tiled=True)  55.6 us
    all_gather x2, blocking collectives, local(): all_tokens = lax.all_gather(hidden, 'col', axis=0, tiled=True)  48.8 us
    all_gather x2, blocking collectives, local(): lax.all_gather(gated, 'row', axis=0, tiled=True)  34.9 us
  transfers between devices with their start and end apart: 9, of which 7 were waited for; matrix products, arithmetic and copies ran while one was open for 8% of the time, Pallas kernels for 0%

commit v1 on v0

--- a/solution.py
+++ b/solution.py
@@ -6,6 +6,12 @@
 S = 16
 SEND_CAP = 2
 EPSILON = 1e-05
+_scan_fields = lambda view, mesh_dim: jnp.concatenate(
+    lax.all_to_all(
+        jnp.stack(lax.axis_size(mesh_dim) * [view], axis=0), mesh_dim, split_axis=0, concat_axis=0
+    ),
+    0,
+)
 
 
 def conv_silu(prefix, incoming, kernel):
@@ -96,7 +102,7 @@
     step_outputs = []
     chosen_layers = []
     for layer_index in range(layer_count):
-        all_tokens = lax.all_gather(hidden, "col", axis=0, tiled=True)
+        all_tokens = _scan_fields(hidden, "col")
         tokens_f = all_tokens.astype(jnp.float32)
         scaled = (tokens_f * input_gain[layer_index]).astype(jnp.bfloat16)
         square_part = jnp.sum(tokens_f * tokens_f, axis=1)

time: 792 us -> 833 us (1.052)
  local copies, waits for them, and re-layouts: 86.9 us -> 123 us
  blocking collectives: 231 us -> 198 us
  other arithmetic: 90.8 us -> 114 us
    all_gather x2 -> x0, blocking collectives: 48.8 us -> none  [local(): all_tokens = lax.all_gather(hidden, 'col', axis=0, tiled=True)]
    all_to_all x0 -> x1, blocking collectives: none -> 14.8 us  [lax.all_to_all(jnp.stack(lax.axis_size(mesh_dim) * [view], axis=0), mesh_...]
    mul x32, other arithmetic: 2.37 us -> 13.8 us  [advance(): delta_now[:, :, None] * value_now]
    dynamic_slice x32, local copies, waits for them, and re-layouts: 0.05 us -> 11 us  [ssm_scan(): last_state, (outputs, states) = lax.scan(advance, start_state, time_major)]
    mul x64, local copies, waits for them, and re-layouts: 13.8 us -> 24.7 us  [advance(): delta_now[:, :, None] * value_now]
    mul x32, local copies, waits for them, and re-layouts: 11.3 us -> 22 us  [advance(): (delta_now[:, :, None] * value_now)[:, :, :, None] * b_now[:, None, None, :]]
    all_to_all x0 -> x1, waiting for transfers between devices: none -> 10.7 us  [lax.all_to_all(jnp.stack(lax.axis_size(mesh_dim) * [view], axis=0), mesh_...]
    dynamic_update_slice x64, other arithmetic: 62.7 us -> 73.2 us  [ssm_scan(): last_state, (outputs, states) = lax.scan(advance, start_state, time_major)]
  transfers between devices with their start and end apart: 9 -> 10, of which waited for: 7 -> 8; matrix products, arithmetic and copies ran while one was open for 8% -> 7% of each run, Pallas kernels for 0% -> 0%
where the time goes in v1:
time: 833 us; the launch traced here: 826 us
  waiting for transfers between devices  258 us (31%)
  blocking collectives  198 us (24%)
  local copies, waits for them, and re-layouts  123 us (15%)
  other arithmetic  114 us (14%)
  matrix products  103 us (12%)
  between operations  15.4 us (2%)
  starting transfers between devices  15.3 us (2%)
    psum x2, blocking collectives, local(): gate_square = lax.psum(jnp.sum(gated_raw * gated_raw, axis=1), 'col')  123 us
    reduce_scatter x2, waiting for transfers between devices, local(): lax.psum_scatter(partial_out.astype(jnp.bfloat16), 'col', scatter_dimensi...  122 us
    dot_general x32, matrix products, advance(): jnp.einsum('rhpn,rn->rhp', updated, c_now, precision=lax.Precision.HIGHEST)  80.9 us
    dynamic_update_slice x64, other arithmetic, ssm_scan(): last_state, (outputs, states) = lax.scan(advance, start_state, time_major)  73.2 us
    reduce_scatter x2, waiting for transfers between devices, local(): lax.psum_scatter(inner_part, 'row', scatter_dimension=0, tiled=True)  67.7 us
    reduce_scatter x2, waiting for transfers between devices, local(): lax.psum_scatter(proj_part, 'row', scatter_dimension=0, tiled=True)  54.4 us
    all_gather x2, blocking collectives, local(): lax.all_gather(gated, 'row', axis=0, tiled=True)  34.7 us
    reshape x2, local copies, waits for them, and re-layouts, local(): states.reshape(token_rows, heads_local * head_size * state_size)  26.6 us
  transfers between devices with their start and end apart: 10, of which 8 were waited for; matrix products, arithmetic and copies ran while one was open for 7% of the time, Pallas kernels for 0%

profile of v1, /device:TPU:0, one launch (start us, length us, event | category | flops | bytes accessed | tf_op | source)
XLA Modules:
  0.0 826.3 jit_solution(9932181819673859142)
XLA Ops:
  8.9 8.0 all-to-all-start
  17.7 10.7 %all-to-all-done = bf16[16,64,256]{2,1,0:T(8,128)(2,1)S(1)} async-done(((bf16[16,64,256]{2,1,0:T(8,128)(2,1)}), bf16[16,64,256]{2,1,0:T(8,128)(2,1)S(1)}, u32[]{:S(2)}, u32[]{:S(2)}) %all-to-all-start) | async-done | bytes 524320 | tf_op jit(solution)/shard_map/all_to_all | solution.py:10
  28.6 1.7 fusion.55
  30.5 2.2 fusion.44
  43.2 13.5 %all-reduce = f32[1024]{0:T(1024)S(1)} all-reduce(f32[1024]{0:T(1024)S(1)} %reduce_sum.50), channel_id=3, replica_groups=mesh['row'=8,'col'=16] {'row'}, use_global_device_ids=true, to_apply=%region_2.0.clone | all-reduce | flops 1024 | bytes 8192
  56.8 2.3 reduce-scatter.25.cloned.1.call-done
  61.6 31.2 %reduce-scatter.15.cloned.1.call-done = f32[128,256]{1,0:T(8,128)} async-done(((f32[1024,256]{1,0:T(8,128)}), f32[128,256]{1,0:T(8,128)}) %reduce-scatter.15.cloned.1.call-update) | async-done | bytes 131088 | tf_op jit(solution)/shard_map/reduce_scatter | solution.py:119
  94.6 33.9 %reduce-scatter.13.cloned.1.call-done = f32[128,512]{1,0:T(8,128)} async-done(((f32[1024,512]{1,0:T(8,128)}), f32[128,512]{1,0:T(8,128)}) %reduce-scatter.13.cloned.1.call-update) | async-done | bytes 262160 | tf_op jit(solution)/shard_map/reduce_scatter | solution.py:117
  130.0 5.4 broadcast.181.clone2
  135.3 92.8 %while.28 = (s32[]{:T(128)}, f32[8,4,64,128]{3,2,1,0:T(8,128)S(1)}, f32[16,8,4,64]{3,2,1,0:T(4,128)S(1)}, bf16[16,8,4,64,128]{4,3,2,0,1:T(8,128)(2,1)}, f32[16,8...) while((s32[]{:T(128)}, f32[8,4,64,128]{3,2,1,0:T(8,128)S(1)}, ...), condition=%wide.region_6.0_spmd, body=%wide.region_5.0_spmd.sunk | while | flops 4200450 | bytes 3778445 | solution.py:46
  138.6 2.5 fusion.99
  144.4 2.5 fusion.99
  150.1 2.5 fusion.99
  155.9 2.5 fusion.99
  161.7 2.5 fusion.99
  167.5 2.5 fusion.99
  173.3 2.5 fusion.99
  179.1 2.5 fusion.99
  185.0 2.5 fusion.99
  190.7 2.5 fusion.99
  196.5 2.5 fusion.99
  202.3 2.5 fusion.99
  208.1 2.5 fusion.99
  213.8 2.5 fusion.99
  219.7 2.5 fusion.99
  225.5 2.5 fusion.99
  228.5 40.6 %psum.14 = f32[128]{0:T(128)S(1)} all-reduce(f32[128]{0:T(128)S(1)} %get-tuple-element.179), channel_id=1, replica_groups=mesh['row'=8,'col'=16] {'col'}, use_global_device_ids=true, to_apply=%region_8.9 | all-reduce | flops 128 | bytes 1024 | tf_op jit(solution)/shard_map/psum | solution.py:151
  269.2 13.1 %all_gather.6 = bf16[1024,256]{1,0:T(8,128)(2,1)S(1)} all-gather(bf16[128,256]{1,0:T(8,128)(2,1)S(1)} %multiply_convert_fusion.1), channel_id=1, replica_groups=mesh['row'=8,'col'=16] {'row'}, dimensions={0}, use_global_device_ids=true | all-gather | bytes 589824 | tf_op jit(solution)/shard_map/all_gather | solution.py:159
  283.5 67.3 %reduce-scatter.17.cloned.1.call-done = bf16[64,256]{1,0:T(8,128)(2,1)} async-done(((bf16[1024,256]{1,0:T(8,128)(2,1)}), bf16[64,256]{1,0:T(8,128)(2,1)}) %reduce-scatter.17.cloned.1.call-update) | async-done | bytes 32784 | tf_op jit(solution)/shard_map/reduce_scatter | solution.py:163
  351.7 14.8 %all_to_all.25 = bf16[16,64,256]{2,1,0:T(8,128)(2,1)S(1)} all-to-all(bf16[16,64,256]{2,1,0:T(8,128)(2,1)S(1)} %stack.13), channel_id=1, replica_groups=mesh['row'=8,'col'=16] {'col'}, dimensions={0} | all-to-all | bytes 1048576 | tf_op jit(solution)/shard_map/all_to_all | solution.py:10
  367.9 2.2 fusion.41
  370.3 1.8 fusion.72
  372.7 13.3 %reshape.335 = bf16[128,32768]{1,0:T(8,128)(2,1)} reshape(bf16[8,16,4,64,128]{4,3,2,1,0:T(8,128)(2,1)} %bitcast.257) | data formatting | bytes 16777216 | tf_op jit(solution)/shard_map/reshape | solution.py:169
  386.0 4.7 fusion.2
  391.2 12.6 %all-reduce.1 = f32[1024]{0:T(1024)S(1)} all-reduce(f32[1024]{0:T(1024)S(1)} %reduce_sum.53), channel_id=8, replica_groups=mesh['row'=8,'col'=16] {'row'}, use_global_device_ids=true, to_apply=%region_12.13.clone | all-reduce | flops 1024 | bytes 8192
  406.4 23.2 %reduce-scatter.21.cloned.1.call-done = f32[128,256]{1,0:T(8,128)} async-done(((f32[1024,256]{1,0:T(8,128)}), f32[128,256]{1,0:T(8,128)}) %reduce-scatter.21.cloned.1.call-update) | async-done | bytes 131088 | tf_op jit(solution)/shard_map/reduce_scatter | solution.py:119
  431.4 33.8 %reduce-scatter.19.cloned.1.call-done = f32[128,512]{1,0:T(8,128)} async-done(((f32[1024,512]{1,0:T(8,128)}), f32[128,512]{1,0:T(8,128)}) %reduce-scatter.19.cloned.1.call-update) | async-done | bytes 262160 | tf_op jit(solution)/shard_map/reduce_scatter | solution.py:117
  468.9 5.4 broadcast.181.clone
  474.3 135.8 %while.29 = (s32[]{:T(128)}, f32[8,4,64,128]{3,2,1,0:T(8,128)S(1)}, f32[16,8,4,64]{3,2,1,0:T(4,128)}, bf16[16,8,4,64,128]{4,3,2,0,1:T(8,128)(2,1)}, f32[16,8,4]{...) while((s32[]{:T(128)}, f32[8,4,64,128]{3,2,1,0:T(8,128)S(1)}, ...), condition=%wide.region_16.17_spmd, body=%wide.region_15.16_spmd.sunk | while | flops 4200450 | bytes 3769757 | solution.py:46
  478.9 2.5 fusion.102
  487.3 2.5 fusion.102
  495.8 2.5 fusion.102
  504.3 2.5 fusion.102
  512.8 2.5 fusion.102
  521.3 2.5 fusion.102
  529.8 2.5 fusion.102
  538.3 2.5 fusion.102
  546.8 2.5 fusion.102
  555.2 2.5 fusion.102
  563.7 2.5 fusion.102
  572.2 2.5 fusion.102
  580.7 2.5 fusion.102
  589.2 2.5 fusion.102
  597.7 2.5 fusion.102
  606.2 2.5 fusion.102
  610.1 13.3 %reshape.336 = bf16[128,32768]{1,0:T(8,128)(2,1)} reshape(bf16[8,16,4,64,128]{4,3,2,1,0:T(8,128)(2,1)} %bitcast.255) | data formatting | bytes 16777216 | tf_op jit(solution)/shard_map/reshape | solution.py:169
  623.4 4.6 fusion.3
  628.5 2.4 pad_maximum_fusion.1
  630.9 7.0 all-to-all-start.2
  638.4 81.9 %psum.15 = f32[128]{0:T(128)S(1)} all-reduce(f32[128]{0:T(128)S(1)} %get-tuple-element.177), channel_id=1, replica_groups=mesh['row'=8,'col'=16] {'col'}, use_global_device_ids=true, to_apply=%region_18.19 | all-reduce | flops 128 | bytes 1024 | tf_op jit(solution)/shard_map/psum | solution.py:151
  720.5 21.6 %all_gather.7 = bf16[1024,256]{1,0:T(8,128)(2,1)S(1)} all-gather(bf16[128,256]{1,0:T(8,128)(2,1)S(1)} %multiply_convert_fusion), channel_id=1, replica_groups=mesh['row'=8,'col'=16] {'row'}, dimensions={0}, use_global_device_ids=true | all-gather | bytes 589824 | tf_op jit(solution)/shard_map/all_gather | solution.py:159
  743.2 13.8 %pad_maximum_fusion = bf16[2,8,16,4,64,128]{5,4,3,2,1,0:T(8,128)(2,1)} fusion(bf16[1,8,16,4,64,128]{5,4,3,2,1,0:T(8,128)(2,1)} %bitcast.256, bf16[1,8,16,4,64,128]{5,4,3,2,1,0:T(8,128)(2,1)} %bitcast.258), kind=kLoop, calls=%fused_computation.22 | loop fusion | flops 8388608 | bytes 33554432 | tf_op jit(solution)/shard_map/stack | solution.py:180
  757.1 55.1 %reduce-scatter.23.cloned.1.call-done = bf16[64,256]{1,0:T(8,128)(2,1)} async-done(((bf16[1024,256]{1,0:T(8,128)(2,1)}), bf16[64,256]{1,0:T(8,128)(2,1)}) %reduce-scatter.23.cloned.1.call-update) | async-done | bytes 32784 | tf_op jit(solution)/shard_map/reduce_scatter | solution.py:163
  813.5 6.0 copy.143
  (408 shorter events, 182.2 us)
Async XLA Ops:
  7.2 28.8 %copy-start.26 = (u32[128]{0:T(128)S(1)}, u32[128]{0:T(128)}, u32[]{:S(2)}) copy-start(u32[128]{0:T(128)} %constant.80) | copy-start | bytes 1540
  7.2 30.0 %copy-start.20 = (f32[2,4]{1,0:T(2,128)S(1)}, f32[2,4]{1,0:T(2,128)}, u32[]{:S(2)}) copy-start(f32[2,4]{1,0:T(2,128)} %param.31) | copy-start | bytes 100
  7.2 30.6 %copy-start.19 = (f32[2,256]{1,0:T(2,128)S(1)}, f32[2,256]{1,0:T(2,128)}, u32[]{:S(2)}) copy-start(f32[2,256]{1,0:T(2,128)} %param.32) | copy-start | bytes 6148
  7.2 31.1 %copy-start.23 = (f32[2,4]{1,0:T(2,128)S(1)}, f32[2,4]{1,0:T(2,128)}, u32[]{:S(2)}) copy-start(f32[2,4]{1,0:T(2,128)} %param.30) | copy-start | bytes 100
  7.2 31.1 %copy-start.22 = (f32[2,4]{1,0:T(2,128)S(1)}, f32[2,4]{1,0:T(2,128)}, u32[]{:S(2)}) copy-start(f32[2,4]{1,0:T(2,128)} %param.29) | copy-start | bytes 100
  7.2 31.7 %copy-start.10 = (f32[2,4,256]{2,1,0:T(4,128)S(1)}, f32[2,4,256]{2,1,0:T(4,128)}, u32[]{:S(2)}) copy-start(f32[2,4,256]{2,1,0:T(4,128)} %param.27) | copy-start | bytes 24580
  7.2 32.3 %copy-start.11 = (f32[2,4,256]{2,1,0:T(4,128)S(1)}, f32[2,4,256]{2,1,0:T(4,128)}, u32[]{:S(2)}) copy-start(f32[2,4,256]{2,1,0:T(4,128)} %param.28) | copy-start | bytes 24580
  7.2 32.9 %copy-start.7 = (bf16[2,8,3,256]{3,1,2,0:T(8,128)(2,1)S(1)}, bf16[2,8,3,256]{3,1,2,0:T(8,128)(2,1)}, u32[]{:S(2)}) copy-start(bf16[2,8,3,256]{3,1,2,0:T(8,128)(2,1)} %param.34) | copy-start | bytes 73732
  7.2 33.5 %copy-start.8 = (bf16[2,8,3,256]{3,1,2,0:T(8,128)(2,1)S(1)}, bf16[2,8,3,256]{3,1,2,0:T(8,128)(2,1)}, u32[]{:S(2)}) copy-start(bf16[2,8,3,256]{3,1,2,0:T(8,128)(2,1)} %param.35) | copy-start | bytes 73732
  8.9 19.5 %all-to-all-start = ((bf16[16,64,256]{2,1,0:T(8,128)(2,1)}), bf16[16,64,256]{2,1,0:T(8,128)(2,1)S(1)}, u32[]{:S(2)}, u32[]{:S(2)}) async-start(bf16[16,64,256]{2,1,0:T(8,128)(2,1)} %stack.12), calls=%async_computation | async-start | bytes 1048576 | tf_op jit(solution)/shard_map/all_to_all | solution.py:10
  16.9 42.3 %reduce-scatter.25.cloned.1.call-start = ((), (), s32[]{:S(2)}) async-start(), calls=%async_computation.17 | async-start | bytes 589824
  30.4 62.4 %reduce-scatter.15.cloned.1.call-start = ((), (), s32[]{:S(2)}) async-start(), calls=%async_computation.12 | async-start | bytes 1179648 | tf_op jit(solution)/shard_map/reduce_scatter | solution.py:119
  32.7 95.9 %reduce-scatter.13.cloned.1.call-start = ((), (), s32[]{:S(2)}) async-start(), calls=%async_computation.11 | async-start | bytes 2359296 | tf_op jit(solution)/shard_map/reduce_scatter | solution.py:117
  35.9 314.9 %reduce-scatter.17.cloned.1.call-start = ((), (), s32[]{:S(2)}) async-start(), calls=%async_computation.13 | async-start | bytes 557056 | tf_op jit(solution)/shard_map/reduce_scatter | solution.py:163
  135.3 147.0 %copy-start.3 = (bf16[2,256,256]{2,1,0:T(8,128)(2,1)S(1)}, bf16[2,256,256]{2,1,0:T(8,128)(2,1)}, u32[]{:S(2)}) copy-start(bf16[2,256,256]{2,1,0:T(8,128)(2,1)} %param.33) | copy-start | bytes 786436
  135.3 215.5 %copy-start.5 = (bf16[64,256]{1,0:T(8,128)(2,1)S(1)}, bf16[64,256]{1,0:T(8,128)(2,1)}, u32[]{:S(2)}) copy-start(bf16[64,256]{1,0:T(8,128)(2,1)} %param.22) | copy-start | bytes 98308
  135.3 231.4 %copy-start.12 = (bf16[2,256,4]{1,2,0:T(4,128)(2,1)S(1)}, bf16[2,256,4]{1,2,0:T(4,128)(2,1)}, u32[]{:S(2)}) copy-start(bf16[2,256,4]{1,2,0:T(4,128)(2,1)} %param.26) | copy-start | bytes 12292
  228.1 144.0 %copy-start.25 = (s32[8]{0:T(128)S(1)}, s32[8]{0:T(128)}, u32[]{:S(2)}) copy-start(s32[8]{0:T(128)} %param.38) | copy-start | bytes 100
  228.1 144.2 %copy-start.21 = (s32[4,2]{0,1:T(2,128)S(1)}, s32[4,2]{0,1:T(2,128)}, u32[]{:S(2)}) copy-start(s32[4,2]{0,1:T(2,128)} %param.39) | copy-start | bytes 100
  228.1 144.2 %copy-start.24 = (s32[8]{0:T(128)S(1)}, s32[8]{0:T(128)}, u32[]{:S(2)}) copy-start(s32[8]{0:T(128)} %param.37) | copy-start | bytes 100
  283.5 120.4 %reduce-scatter.27.cloned.1.call-start = ((), (), s32[]{:S(2)}) async-start(), calls=%async_computation.18 | async-start | bytes 589824
  351.6 14.9 %copy-start.1 = (bf16[64,256]{1,0:T(8,128)(2,1)}, bf16[64,256]{1,0:T(8,128)(2,1)S(1)}, u32[]{:S(2)}) copy-start(bf16[64,256]{1,0:T(8,128)(2,1)S(1)} %add_convert_fusion.1) | copy-start | bytes 98308
  367.9 61.7 %reduce-scatter.21.cloned.1.call-start = ((), (), s32[]{:S(2)}) async-start(), calls=%async_computation.15 | async-start | bytes 1179648 | tf_op jit(solution)/shard_map/reduce_scatter | solution.py:119
  370.2 95.0 %reduce-scatter.19.cloned.1.call-start = ((), (), s32[]{:S(2)}) async-start(), calls=%async_computation.14 | async-start | bytes 2359296 | tf_op jit(solution)/shard_map/reduce_scatter | solution.py:117
  386.0 18.9 %copy-start.17 = (f32[4]{0:T(128)S(1)}, f32[4]{0:T(128)}, u32[]{:S(2)}) copy-start(f32[4]{0:T(128)} %get-tuple-element.229) | copy-start | bytes 52
  386.0 18.9 %copy-start.18 = (f32[4]{0:T(128)S(1)}, f32[4]{0:T(128)}, u32[]{:S(2)}) copy-start(f32[4]{0:T(128)} %get-tuple-element.233) | copy-start | bytes 52
  386.0 44.7 %copy-start.6 = (f32[8,3,256]{2,0,1:T(8,128)S(1)}, f32[8,3,256]{2,0,1:T(8,128)}, u32[]{:S(2)}) copy-start(f32[8,3,256]{2,0,1:T(8,128)} %get-tuple-element.197) | copy-start | bytes 73732
  386.0 44.7 %copy-start.13 = (f32[1,1,256]{2,1,0:T(1,128)S(1)}, f32[1,1,256]{2,1,0:T(1,128)}, u32[]{:S(2)}) copy-start(f32[1,1,256]{2,1,0:T(1,128)} %get-tuple-element.206) | copy-start | bytes 3076
  386.0 44.7 %copy-start.14 = (f32[1,1,256]{2,1,0:T(1,128)S(1)}, f32[1,1,256]{2,1,0:T(1,128)}, u32[]{:S(2)}) copy-start(f32[1,1,256]{2,1,0:T(1,128)} %get-tuple-element.211) | copy-start | bytes 3076
  386.0 44.7 %copy-start.15 = (f32[1,1,256]{2,1,0:T(1,128)S(1)}, f32[1,1,256]{2,1,0:T(1,128)}, u32[]{:S(2)}) copy-start(f32[1,1,256]{2,1,0:T(1,128)} %get-tuple-element.212) | copy-start | bytes 3076
  468.1 6.2 copy-start.9
  628.5 9.5 %copy-start = (f32[16,8,4,64]{3,2,1,0:T(4,128)S(1)}, f32[16,8,4,64]{3,2,1,0:T(4,128)}, u32[]{:S(2)}) copy-start(f32[16,8,4,64]{3,2,1,0:T(4,128)} %get-tuple-element.110) | copy-start | bytes 393220
  628.5 91.9 %copy-start.16 = (f32[1,256]{1,0:T(1,128)S(1)}, f32[1,256]{1,0:T(1,128)}, u32[]{:S(2)}) copy-start(f32[1,256]{1,0:T(1,128)} %get-tuple-element.221) | copy-start | bytes 3076
  628.5 113.6 %copy-start.4 = (bf16[2,256,256]{2,1,0:T(8,128)(2,1)S(1)}, bf16[2,256,256]{2,1,0:T(8,128)(2,1)}, u32[]{:S(2)}) copy-start(bf16[2,256,256]{2,1,0:T(8,128)(2,1)} %param.33) | copy-start | bytes 786436
  630.9 182.6 %all-to-all-start.2 = ((bf16[16,2,2,4,64,128]{5,4,3,1,2,0:T(8,128)(2,1)}), bf16[16,2,2,4,64,128]{5,4,3,1,2,0:T(8,128)(2,1)}, u32[]{:S(2)}, u32[]{:S(2)}) async-start(bf16[16,2,2,4,64,128]{5,4,3,1,2,0:T(8,128)(2,1)} %pad_maximum_fusion.1), calls=%async_computation.8 | async-start | bytes 8388608 | tf_op jit(solution)/shard_map/all_to_all | solution.py:176
  638.0 174.1 %reduce-scatter.23.cloned.1.call-start = ((), (), s32[]{:S(2)}) async-start(), calls=%async_computation.16 | async-start | bytes 557056 | tf_op jit(solution)/shard_map/reduce_scatter | solution.py:163
  743.2 68.9 %copy-start.2 = (bf16[64,256]{1,0:T(8,128)(2,1)S(1)}, bf16[64,256]{1,0:T(8,128)(2,1)}, u32[]{:S(2)}) copy-start(bf16[64,256]{1,0:T(8,128)(2,1)} %copy-done.1) | copy-start | bytes 98308
Sparse Core Ops, SparseCore 0:
  30.5 28.5 reduce-scatter.24
  62.2 30.5 reduce-scatter.14
  96.0 32.5 reduce-scatter.12
  283.6 67.2 reduce-scatter.16
  368.0 28.3 reduce-scatter.26
  398.8 30.7 reduce-scatter.20
  432.7 32.4 reduce-scatter.18
  743.3 68.7 reduce-scatter.22
